TPU v7x, 256 devices: a whole 4x4x8 slice. The times are simulated.
256 devices in a mesh: task: 8 (over z_hi, core), row: 8 (over x, z_lo), col: 4 (over y).
Axes of the slice: x: 4, y: 4, z: 8 (z_hi: 4, z_lo: 2; z = z_hi * 2 + z_lo), core: 2. Of those that a mesh axis runs over, the one named last changes fastest.
Arguments:
- activations: bfloat16 [8, 512, 13824], P('task', 'col', 'row'), may hold values from -6 to 6
- weights: bfloat16 [8, 13824, 5120], P('task', 'row', 'col'), may hold values from -0.0625 to 0.0625
- labels: int32 [8, 512], P('task'), may hold values from 0 to 127
- prototypes: bfloat16 [8, 128, 5120], P('task', None, 'col'), may hold values from -6 to 6
Outputs:
- merged: bfloat16 [13824, 5120], P('row', 'col')
- merged_out: bfloat16 [8, 512, 5120], P('task', 'row', 'col')
All inputs are finite; a program needn't handle non-finite values.
Results may differ from a plain program's by a relative error of at most 0.02.
Values may be sent and summed in bfloat16 or wider, within the bound.
A program may use at most 128 MiB of HBM per device.

v0:
```python
import jax
import jax.numpy as jnp
from jax import lax
from jax.sharding import PartitionSpec as P


def class_targets(label_rows, protos):
    count = label_rows.shape[0]
    onehot = (
        label_rows[:, None] == lax.broadcasted_iota(jnp.int32, (count, protos.shape[0]), 1)
    ).astype(jnp.bfloat16)
    return jnp.dot(onehot, protos, preferred_element_type=jnp.float32)


def local(activations, weights, labels, prototypes):
    acts = activations[0]
    weight = weights[0]
    label_row = labels[0]
    protos = prototypes[0]
    full_acts = lax.all_gather(acts, "col", axis=0, tiled=True)
    partial_out = jnp.dot(full_acts, weight, preferred_element_type=jnp.float32)
    output = lax.psum(partial_out.astype(jnp.bfloat16), "row").astype(jnp.float32)
    grad = output - class_targets(label_row, protos)
    gsq = (grad * grad).astype(jnp.bfloat16)
    wide = full_acts.astype(jnp.float32)
    asq = (wide * wide).astype(jnp.bfloat16)
    fisher = lax.dot_general(asq, gsq, (((0,), (0,)), ((), ())), preferred_element_type=jnp.float32)
    weighted = fisher * weight.astype(jnp.float32)
    numer, denom = (
        lax.psum_scatter(weighted, "task", scatter_dimension=0, tiled=True),
        lax.psum_scatter(fisher, "task", scatter_dimension=0, tiled=True),
    )
    piece = (numer / (denom + 1e-06)).astype(jnp.bfloat16)
    merged = lax.all_gather(piece, "task", axis=0, tiled=True)
    result = lax.psum_scatter(
        jnp.dot(full_acts, merged, preferred_element_type=jnp.float32).astype(jnp.bfloat16),
        "row",
        scatter_dimension=0,
        tiled=True,
    )
    return (merged, result[None])


def solution(mesh):
    placed = (
        P("task", "col", "row"),
        P("task", "row", "col"),
        P("task", None),
        P("task", None, "col"),
    )
    return jax.shard_map(
        local,
        mesh=mesh,
        in_specs=placed,
        out_specs=(P("row", "col"), P("task", "row", "col")),
        check_vma=False,
    )
```

profile of v0, /device:TPU:8, one launch (start us, length us, event | category | flops | bytes accessed | tf_op | source)
XLA Modules:
  0.0 475.8 jit_solution(1805810077636972893)
XLA Ops:
  7.2 0.0 copy-start
  7.2 0.0 all-gather.6.cloned.1.call-start
  7.2 0.7 all-gather.6.cloned.1.call-update
  7.9 0.0 copy-start.2
  7.9 0.0 all-reduce.2.cloned.1.call-start
  8.0 38.4 %all-gather.6.cloned.1.call-done = bf16[1,512,1728]{1,2,0:T(8,128)(2,1)} async-done(((bf16[1,128,1728]{1,2,0:T(8,128)(2,1)}), bf16[1,512,1728]{1,2,0:T(8,128)(2,1)}) %all-gather.6.cloned.1.call-update) | async-done | bytes 1769488 | tf_op jit(solution)/shard_map/all_gather | solution.py:20
  46.4 0.0 copy-start.1
  46.4 6.6 %fusion.4 = bf16[512,1280]{1,0:T(8,128)(2,1)} fusion(bf16[1,1728,1280]{2,1,0:T(8,128)(2,1)} %param.5, bf16[1,512,1728]{1,2,0:T(8,128)(2,1)} %all-gather.6.cloned.1.call-done), kind=kOutput, calls=%fused_computation.7 | convolution fusion | flops 2265579520 | bytes 7503872 | tf_op jit(solution)/shard_map/dot_general | solution.py:21
  53.0 0.0 all-reduce.2.cloned.1.call-update
  53.0 0.0 reduce-scatter.6.cloned.1.call-start
  53.1 90.5 %all-reduce.2.cloned.1.call-done = bf16[512,1280]{1,0:T(8,128)(2,1)} async-done(((bf16[512,1280]{1,0:T(8,128)(2,1)}), bf16[512,1280]{1,0:T(8,128)(2,1)}) %all-reduce.2.cloned.1.call-update) | async-done | bytes 1310736 | tf_op jit(solution)/shard_map/psum | solution.py:22
  143.6 0.0 copy-done
  143.6 0.0 copy-done.2
  143.6 0.0 copy-done.1
  143.6 9.8 %convert_multiply_fusion = (f32[1728,1280]{1,0:T(8,128)}, f32[1728,1280]{1,0:T(8,128)}) fusion(bf16[1,1728,1280]{2,1,0:T(8,128)(2,1)} %param.5, bf16[512,1280]{1,0:T(8,128)(2,1)} %all-reduce.2.cloned.1.call-done, bf16[1,128,1280]{2,1,0:T(8,128)(2,1)S(1)} %copy-done, s32[512]{0:T(512)S(1)} %bitcast.30, bf16[1,512,1728]{1,2,0:T(8,128)(2,1)S(1)} %copy-done.1), kind=kOutput, calls=%fused_computation | convolution fusion | flops 2442461184 | bytes 25528320 | tf_op jit(solution)/shard_map/dot_general | solution.py:27
  153.4 0.0 reduce-scatter.6.cloned.1.call-update
  153.4 0.0 reduce-scatter.8.cloned.1.call-start
  153.4 0.5 reduce-scatter.8.cloned.1.call-update
  154.0 0.0 all-gather.4.cloned.1.call-start
  154.0 96.8 %reduce-scatter.6.cloned.1.call-done = f32[216,1280]{1,0:T(8,128)} async-done(((f32[1728,1280]{1,0:T(8,128)}), f32[216,1280]{1,0:T(8,128)}) %reduce-scatter.6.cloned.1.call-update) | async-done | bytes 1105936 | tf_op jit(solution)/shard_map/reduce_scatter | solution.py:30
  250.8 104.8 %reduce-scatter.8.cloned.1.call-done = f32[216,1280]{1,0:T(8,128)} async-done(((f32[1728,1280]{1,0:T(8,128)}), f32[216,1280]{1,0:T(8,128)}) %reduce-scatter.8.cloned.1.call-update) | async-done | bytes 1105936 | tf_op jit(solution)/shard_map/reduce_scatter | solution.py:31
  355.7 2.5 divide_convert_fusion
  358.2 0.0 all-gather.4.cloned.1.call-update
  358.2 0.0 reduce-scatter.10.cloned.1.call-start
  358.3 54.9 %all-gather.4.cloned.1.call-done = bf16[1728,1280]{1,0:T(8,128)(2,1)} async-done(((bf16[216,1280]{1,0:T(8,128)(2,1)}), bf16[1728,1280]{1,0:T(8,128)(2,1)}) %all-gather.4.cloned.1.call-update) | async-done | bytes 4423696 | tf_op jit(solution)/shard_map/all_gather | solution.py:34
  413.1 4.8 %fusion.7 = bf16[512,1280]{0,1:T(8,128)(2,1)S(1)} fusion(bf16[1728,1280]{1,0:T(8,128)(2,1)} %all-gather.4.cloned.1.call-done, bf16[1,512,1728]{1,2,0:T(8,128)(2,1)S(1)} %copy-done.1), kind=kOutput, calls=%fused_computation.9 | convolution fusion | flops 2265579520 | bytes 7503872 | tf_op jit(solution)/shard_map/dot_general | solution.py:36
  418.0 1.4 copy.8
  419.4 0.0 reduce-scatter.10.cloned.1.call-update
  419.4 42.9 %reduce-scatter.10.cloned.1.call-done = bf16[64,1280]{1,0:T(8,128)(2,1)} async-done(((bf16[512,1280]{1,0:T(8,128)(2,1)}), bf16[64,1280]{1,0:T(8,128)(2,1)}) %reduce-scatter.10.cloned.1.call-update) | async-done | bytes 163856
  462.4 1.1 copy.9
  463.5 0.8 copy.7
  464.3 4.6 copy.12
Async XLA Ops:
  7.2 136.4 %copy-start = (bf16[1,128,1280]{2,1,0:T(8,128)(2,1)S(1)}, bf16[1,128,1280]{2,1,0:T(8,128)(2,1)}, u32[]{:S(2)}) copy-start(bf16[1,128,1280]{2,1,0:T(8,128)(2,1)} %param.7) | copy-start | bytes 983044
  7.2 39.2 %all-gather.6.cloned.1.call-start = ((), (), s32[]{:S(2)}) async-start(), calls=%async_computation.7 | async-start | bytes 2211840 | tf_op jit(solution)/shard_map/all_gather | solution.py:20
  7.9 135.7 %copy-start.2 = (s32[1,512]{1,0:T(1,128)S(1)}, s32[1,512]{1,0:T(1,128)}, u32[]{:S(2)}) copy-start(s32[1,512]{1,0:T(1,128)} %param.6) | copy-start | bytes 6148
  7.9 135.7 %all-reduce.2.cloned.1.call-start = ((), (), s32[]{:S(2)}) async-start(), calls=%async_computation.3 | async-start | bytes 2621440 | tf_op jit(solution)/shard_map/psum | solution.py:22
  46.4 97.2 %copy-start.1 = (bf16[1,512,1728]{1,2,0:T(8,128)(2,1)S(1)}, bf16[1,512,1728]{1,2,0:T(8,128)(2,1)}, u32[]{:S(2)}) copy-start(bf16[1,512,1728]{1,2,0:T(8,128)(2,1)} %all-gather.6.cloned.1.call-done) | copy-start | bytes 5308420
  53.0 197.8 %reduce-scatter.6.cloned.1.call-start = ((), (), s32[]{:S(2)}) async-start(), calls=%async_computation.4 | async-start | bytes 9953280 | tf_op jit(solution)/shard_map/reduce_scatter | solution.py:30
  153.4 202.3 %reduce-scatter.8.cloned.1.call-start = ((), (), s32[]{:S(2)}) async-start(), calls=%async_computation.5 | async-start | bytes 9953280 | tf_op jit(solution)/shard_map/reduce_scatter | solution.py:31
  154.0 259.2 %all-gather.4.cloned.1.call-start = ((), (), s32[]{:S(2)}) async-start(), calls=%async_computation.6 | async-start | bytes 4976640 | tf_op jit(solution)/shard_map/all_gather | solution.py:34
  358.2 104.1 %reduce-scatter.10.cloned.1.call-start = ((), (), s32[]{:S(2)}) async-start(), calls=%async_computation.8 | async-start | bytes 1474560
Sparse Core Ops, SparseCore 0:
  9.8 36.5 all-gather.5
  53.1 90.4 all-reduce.1
  153.5 97.2 reduce-scatter.5
  253.4 102.1 reduce-scatter.7
  358.3 54.7 all-gather.3
  419.6 42.7 reduce-scatter.9
where the time goes:
time: 476 us
  waiting for transfers between devices  430 us (90%)
  matrix products  21.2 us (4%)
  between operations  14.1 us (3%)
  local copies, waits for them, and re-layouts  8.06 us (2%)
    reduce_scatter x1, waiting for transfers between devices, local(): lax.psum_scatter(fisher, 'task', scatter_dimension=0, tiled=True)  105 us
    reduce_scatter x1, waiting for transfers between devices, local(): lax.psum_scatter(weighted, 'task', scatter_dimension=0, tiled=True)  96.8 us
    psum x1, waiting for transfers between devices, local(): lax.psum(partial_out.astype(jnp.bfloat16), 'row').astype(jnp.float32)  90.5 us
    all_gather x1, waiting for transfers between devices, local(): merged = lax.all_gather(piece, 'task', axis=0, tiled=True)  54.9 us
    unnamed x7, waiting for transfers between devices  44.2 us
    all_gather x1, waiting for transfers between devices, local(): full_acts = lax.all_gather(acts, 'col', axis=0, tiled=True)  38.4 us
    dot_general x1, matrix products, local(): lax.dot_general(asq, gsq, (((0,), (0,)), ((), ())), preferred_element_typ...  9.77 us
  transfers between devices with their start and end apart: 6, of which 6 were waited for; matrix products, arithmetic and copies ran while one was open for 0% of the time, Pallas kernels for 0%

commit v1 on v0

v1 whole, which is shorter than its diff:
```python
import functools

import jax
import jax.numpy as jnp
from jax import lax
from jax.experimental import pallas as pl
from jax.experimental.pallas import tpu as pltpu
from jax.sharding import PartitionSpec as P

MESH = pl.DeviceIdType.MESH
F32, BF16 = jnp.float32, jnp.bfloat16
ZH, XS, YS = 4, 4, 4
CW = 256
HALF = CW // 2

X1, Z1, Z2, X2, CORE, FAR, NEAR, SUM, MERGED, FORWARD, SHARE, X3, Z3 = 0, 3, 4, 5, 8, 9, 11, 13, 15, 17, 18, 22, 25
SLOTS = 26


def kernel(
    chunks, acts_in, w_in, labels, protos, merged_out, out,
    acts, w, asq_t, target, part, part_in, row_sum, z_send, z_in, gsq, nd, nd_in, nd_sum,
    far_in, near_in, sum_in, merged, part2, part2_in, row_sum2, z_send2, z_in2,
    send_sem, recv_sem, gather_send, gather_recv, local_sem, store_sem,
):
    task, row, y = lax.axis_index("task"), lax.axis_index("row"), lax.axis_index("col")
    zh, core = task // 2, task % 2
    x, zl = row // 2, row % 2
    tok, units = acts.shape
    block = tok // XS
    half = block // 2
    piece = units // ZH

    def at_x(step):
        return {"row": (x + step) % XS * 2 + zl}

    pair = {"row": x * 2 + 1 - zl}
    twin = {"task": zh * 2 + 1 - core}

    def at_z(step):
        return {"task": (zh + step + ZH) % ZH * 2 + core}

    def at_y(step):
        return {"col": (y + step + YS) % YS}

    def rows_of(index, size):
        return pl.ds(pl.multiple_of(index * size, size), size)

    def z_piece(step):
        return rows_of((zh + step + ZH) % ZH, piece)

    mine = pl.ds(pl.multiple_of(core * HALF, HALF), HALF)
    others = pl.ds(pl.multiple_of((1 - core) * HALF, HALF), HALF)

    def remote(src, dst, c, slot, device):
        return pltpu.make_async_remote_copy(
            src_ref=src, dst_ref=dst, send_sem=send_sem.at[c, slot], recv_sem=recv_sem.at[c, slot],
            device_id=device, device_id_type=MESH,
        )

    def x1(c, d):
        return remote(part.at[c, rows_of((x + d) % XS, block)], part_in.at[c, d - 1], c, X1 + d - 1, at_x(d))

    def z1(c):
        return remote(z_send.at[c], z_in.at[c], c, Z1, pair)

    def z2(c):
        here = gsq.at[c, rows_of(row, half)]
        return remote(here, here, c, Z2, pair)

    def x2(c, d):
        here = gsq.at[c, rows_of(x, block)]
        return remote(here, here, c, X2 + d - 1, at_x(d))

    def across(c):
        return remote(nd.at[c, :, :, others], nd_in.at[c], c, CORE, twin)

    def far(c, k):
        return remote(nd_sum.at[c, k, z_piece(2)], far_in.at[c, k], c, FAR + k, at_z(1 - 2 * k))

    def near(c, k):
        return remote(nd_sum.at[c, 1 - k, z_piece(1 - 2 * k)], near_in.at[c, k], c, NEAR + k, at_z(1 - 2 * k))

    def summed(c, k):
        return remote(nd_sum.at[c, k, z_piece(1 - 2 * k)], sum_in.at[c, k], c, SUM + k, at_z(1 - 2 * k))

    def spread(c, k):
        here = merged.at[c, z_piece(0), mine]
        return remote(here, here, c, MERGED + k, at_z(1 - 2 * k))

    def forward(c):
        here = merged.at[c, z_piece(2 * core - 1), mine]
        return remote(here, here, c, FORWARD, at_z(1 - 2 * core))

    def share(c, step):
        here = merged.at[c, z_piece(step), mine]
        return remote(here, here, c, SHARE + step, twin)

    def x3(c, d):
        return remote(part2.at[c, rows_of((x + d) % XS, block)], part2_in.at[c, d - 1], c, X3 + d - 1, at_x(d))

    def z3(c):
        return remote(z_send2.at[c], z_in2.at[c], c, Z3, pair)

    def store(c):
        return pltpu.make_async_copy(
            merged.at[c], merged_out.at[:, pl.ds(pl.multiple_of(c * CW, CW), CW)], store_sem.at[c]
        )

    own = rows_of(y, block)
    load_acts = pltpu.make_async_copy(acts_in, acts.at[own], local_sem.at[chunks])
    load_acts.start()
    loads = [
        pltpu.make_async_copy(w_in.at[:, pl.ds(c * CW, CW)], w.at[c], local_sem.at[c]) for c in range(chunks)
    ]
    for load in loads:
        load.start()

    barrier = pltpu.get_barrier_semaphore()
    peers = [at_y(1), at_y(-1), at_x(1), at_x(2), at_x(3), pair, twin, at_z(1), at_z(-1)]
    for peer in peers:
        pl.semaphore_signal(barrier, inc=1, device_id=peer, device_id_type=MESH)
    pl.semaphore_wait(barrier, len(peers))

    def gather(src, index, slot, device):
        return pltpu.make_async_remote_copy(
            src_ref=src, dst_ref=acts.at[rows_of(index, block)], send_sem=gather_send.at[slot],
            recv_sem=gather_recv.at[slot], device_id=device, device_id_type=MESH,
        )

    up, down = gather(acts_in, y, 0, at_y(1)), gather(acts_in, y, 1, at_y(-1))
    up.start()
    down.start()

    onehot = (
        labels[rows_of(row, half), :] == lax.broadcasted_iota(jnp.int32, (half, protos.shape[0]), 1)
    ).astype(F32).astype(BF16)
    target[...] = jnp.dot(onehot, protos[...], preferred_element_type=F32)

    def square(index):
        wide = acts[rows_of(index, block), :].astype(F32)
        asq_t[:, rows_of(index, block)] = (wide * wide).T.astype(BF16)

    load_acts.wait()
    square(y)
    up.wait_recv()
    down.wait_recv()
    source = (y + 2 * core - 1 + YS) % YS
    onward = gather(acts.at[rows_of(source, block)], source, 2, at_y(1 - 2 * core))
    onward.start()
    square((y + 1) % YS)
    square((y + 3) % YS)
    onward.wait_recv()
    square((y + 2) % YS)
    for load in loads:
        load.wait()

    def product(left, c, right, result):
        for m in range(2):
            rows = pl.ds(m * (tok // 2), tok // 2)
            result[c, rows, :] = jnp.dot(left[rows, :], right[c], preferred_element_type=F32).astype(BF16)

    def reduce_x(c, own_part, arrived, start):
        rows = pl.ds(pl.multiple_of(start, half), half)
        total = own_part[c, pl.ds(pl.multiple_of(x * block + start, half), half), :].astype(F32)
        for d in range(XS - 1):
            total = total + arrived[c, d, rows, :].astype(F32)
        return total

    def s1(c):
        product(acts, c, w, part)
        for d in (1, 2, 3):
            x1(c, d).start()

    def s2(c):
        for d in (1, 2, 3):
            x1(c, d).wait_recv()
        z_send[c] = reduce_x(c, part, part_in, (1 - zl) * half).astype(BF16)
        z1(c).start()
        row_sum[c] = reduce_x(c, part, part_in, zl * half)

    def s3(c):
        z1(c).wait_recv()
        grad = row_sum[c] + z_in[c].astype(F32) - target[:, pl.ds(pl.multiple_of(c * CW, CW), CW)]
        gsq[c, rows_of(row, half), :] = (grad * grad).astype(BF16)
        z2(c).start()

    def s4(c):
        z2(c).wait_recv()
        for d in (1, 2, 3):
            x2(c, d).start()

    def s5(c):
        for d in (1, 2, 3):
            x2(c, d).wait_recv()
        for q in range(ZH):
            rows = pl.ds(q * piece, piece)
            fisher = jnp.dot(asq_t[rows, :], gsq[c], preferred_element_type=F32)
            nd[c, 0, rows, :] = (fisher * w[c, rows, :].astype(F32)).astype(BF16)
            nd[c, 1, rows, :] = fisher.astype(BF16)
        across(c).start()

    def s6(c):
        across(c).wait_recv()

        def add(k, step):
            rows = z_piece(step)
            nd_sum[c, k, rows, :] = (nd[c, k, rows, mine].astype(F32) + nd_in[c, k, rows, :].astype(F32)).astype(BF16)

        add(0, 2)
        far(c, 0).start()
        add(1, 2)
        far(c, 1).start()
        add(1, 1)
        near(c, 0).start()
        add(0, -1)
        near(c, 1).start()
        add(0, 1)
        add(1, -1)
        add(0, 0)
        add(1, 0)

    def s7(c):
        for k in range(2):
            far(c, k).wait_recv()
            rows = z_piece(1 - 2 * k)
            nd_sum[c, k, rows, :] = (nd_sum[c, k, rows, :].astype(F32) + far_in[c, k].astype(F32)).astype(BF16)
            summed(c, k).start()

    def s8(c):
        for k in range(2):
            near(c, k).wait_recv()
            summed(c, k).wait_recv()
        rows = z_piece(0)
        numer = nd_sum[c, 0, rows, :].astype(F32) + near_in[c, 1].astype(F32) + sum_in[c, 0].astype(F32)
        denom = nd_sum[c, 1, rows, :].astype(F32) + near_in[c, 0].astype(F32) + sum_in[c, 1].astype(F32)
        merged[c, rows, mine] = (numer / (denom + 1e-6)).astype(BF16)
        spread(c, 0).start()
        spread(c, 1).start()
        share(c, 0).start()

    def s9(c):
        spread(c, 0).wait_recv()
        spread(c, 1).wait_recv()
        forward(c).start()
        share(c, 1).start()
        share(c, 3).start()

    def s10(c):
        forward(c).wait_recv()
        share(c, 2).start()

    def s11(c):
        for step in range(ZH):
            share(c, step).wait_recv()
        product(acts, c, merged, part2)
        for d in (1, 2, 3):
            x3(c, d).start()
        store(c).start()

    def s12(c):
        for d in (1, 2, 3):
            x3(c, d).wait_recv()
        z_send2[c] = reduce_x(c, part2, part2_in, (1 - zl) * half).astype(BF16)
        z3(c).start()
        row_sum2[c] = reduce_x(c, part2, part2_in, zl * half)

    def s13(c):
        z3(c).wait_recv()
        out[:, pl.ds(pl.multiple_of(c * CW, CW), CW)] = (row_sum2[c] + z_in2[c].astype(F32)).astype(BF16)

    stages = [s1, s2, s3, s4, s5, s6, s7, s8, s9, s10, s11, s12, s13]

    @pl.loop(0, chunks + len(stages) - 1)
    def _(tick):
        for k in reversed(range(len(stages))):
            c = tick - k

            @pl.when((c >= 0) & (c < chunks))
            def _():
                stages[k](c)

    up.wait_send()
    down.wait_send()
    onward.wait_send()

    @pl.loop(0, chunks)
    def _(c):
        for d in (1, 2, 3):
            x1(c, d).wait_send()
            x2(c, d).wait_send()
            x3(c, d).wait_send()
        for copy in (z1, z2, z3, across, forward):
            copy(c).wait_send()
        for k in range(2):
            for copy in (far, near, summed, spread):
                copy(c, k).wait_send()
        for step in range(ZH):
            share(c, step).wait_send()
        store(c).wait()


def local(activations, weights, labels, prototypes):
    shard, units = activations.shape[1:]
    tok, wide = labels.shape[1], weights.shape[2]
    chunks, block, half, piece = wide // CW, tok // XS, tok // XS // 2, units // ZH

    def vmem(*shape, kind=BF16):
        return pltpu.VMEM(shape, kind)

    anywhere = pl.BlockSpec(memory_space=pl.ANY)
    inside = pl.BlockSpec(memory_space=pltpu.VMEM)
    merged, result = pl.pallas_call(
        functools.partial(kernel, chunks),
        out_shape=(
            jax.ShapeDtypeStruct((units, wide), BF16),
            jax.ShapeDtypeStruct((half, wide), BF16),
        ),
        in_specs=[anywhere, anywhere, inside, inside],
        out_specs=(anywhere, inside),
        scratch_shapes=[
            vmem(tok, units),
            vmem(chunks, units, CW),
            vmem(units, tok),
            vmem(half, wide, kind=F32),
            vmem(chunks, tok, CW),
            vmem(chunks, XS - 1, block, CW),
            vmem(chunks, half, CW, kind=F32),
            vmem(chunks, half, CW),
            vmem(chunks, half, CW),
            vmem(chunks, tok, CW),
            vmem(chunks, 2, units, CW),
            vmem(chunks, 2, units, HALF),
            vmem(chunks, 2, units, HALF),
            vmem(chunks, 2, piece, HALF),
            vmem(chunks, 2, piece, HALF),
            vmem(chunks, 2, piece, HALF),
            vmem(chunks, units, CW),
            vmem(chunks, tok, CW),
            vmem(chunks, XS - 1, block, CW),
            vmem(chunks, half, CW, kind=F32),
            vmem(chunks, half, CW),
            vmem(chunks, half, CW),
            pltpu.SemaphoreType.DMA((chunks, SLOTS)),
            pltpu.SemaphoreType.DMA((chunks, SLOTS)),
            pltpu.SemaphoreType.DMA((3,)),
            pltpu.SemaphoreType.DMA((3,)),
            pltpu.SemaphoreType.DMA((chunks + 1,)),
            pltpu.SemaphoreType.DMA((chunks,)),
        ],
        compiler_params=pltpu.CompilerParams(
            collective_id=0, has_side_effects=True, vmem_limit_bytes=60 << 20
        ),
    )(activations[0], weights[0], labels.reshape(tok, 1), prototypes[0])
    return merged, result[None]


def solution(mesh):
    placed = (
        P("task", "col", "row"),
        P("task", "row", "col"),
        P("task", None),
        P("task", None, "col"),
    )
    return jax.shard_map(
        local,
        mesh=mesh,
        in_specs=placed,
        out_specs=(P("row", "col"), P("task", "row", "col")),
        check_vma=False,
    )
```

time: 476 us -> 197 us (0.41)
  waiting for transfers between devices: 430 us -> 0 us
  Pallas kernels: 0 us -> 184 us
  matrix products: 21.2 us -> 0 us
  between operations: 14.1 us -> 0.65 us
    reduce_scatter x2 -> x0, waiting for transfers between devices: 202 us -> none  [the longest x1 105 us: local(): lax.psum_scatter(fisher, 'task', scatter_dimension=0, tiled=True)]
    pallas_call x0 -> x1, Pallas kernels: none -> 184 us  [local(): pl.pallas_call(functools.partial(kernel, chunks), out_shape=(jax.ShapeDty...]
    all_gather x2 -> x0, waiting for transfers between devices: 93.3 us -> none  [the longest x1 54.9 us: local(): merged = lax.all_gather(piece, 'task', axis=0, tiled=True)]
    psum x1 -> x0, waiting for transfers between devices: 90.5 us -> none  [local(): lax.psum(partial_out.astype(jnp.bfloat16), 'row').astype(jnp.float32)]
    unnamed x7 -> x0, waiting for transfers between devices: 44.2 us -> none
    dot_general x3 -> x0, matrix products: 21.2 us -> none  [the longest x1 9.77 us: local(): lax.dot_general(asq, gsq, (((0,), (0,)), ((), ())), preferred_element_typ...]
  transfers between devices with their start and end apart: 6 -> 0, of which waited for: 6 -> 0; matrix products, arithmetic and copies ran while one was open for 0% -> 0% of each run, Pallas kernels for 0% -> 0%
where the time goes in v1:
time: 197 us; the launch traced here: 193 us
  Pallas kernels  184 us (93%)
  local copies, waits for them, and re-layouts  8.85 us (4%)
    pallas_call x1, Pallas kernels, local(): pl.pallas_call(functools.partial(kernel, chunks), out_shape=(jax.ShapeDty...  184 us
    unnamed x5, local copies, waits for them, and re-layouts  7.32 us

profile of v1, /device:TPU:8, one launch (start us, length us, event | category | flops | bytes accessed | tf_op | source)
XLA Modules:
  0.0 193.2 jit_solution(14050021137920504780)
XLA Ops:
  0.6 1.5 copy.8.labels
  2.2 2.0 %copy.7 = bf16[1,128,1728]{2,1,0:T(8,128)(2,1)} copy(bf16[1,128,1728]{1,2,0:T(8,128)(2,1)} %param.4) | data formatting | bytes 884736 | tf_op args[0]
  4.1 183.7 %shard_map.59 = (bf16[1728,1280]{1,0:T(8,128)(2,1)}, bf16[64,1280]{1,0:T(8,128)(2,1)}) custom-call(bf16[128,1728]{1,0:T(8,128)(2,1)} %bitcast.6, bf16[1728,1280]{1,0:T(8,128)(2,1)} %bitcast.5, s32[512,1]{1,0:T(8,128)} %copy.8.labels, bf16[128,1280]{1,0:T(8,128)(2,1)} %bitcast.7), custom_call_target="tpu_custom_call" | custom-call | tf_op jit(solution)/shard_map/pallas_call | solution.py:313
  187.9 0.0 copy-start
  187.9 4.7 %copy.11 = bf16[1728,1280]{1,0:T(8,128)(2,1)} copy(bf16[1728,1280]{1,0:T(8,128)(2,1)} %get-tuple-element.8) | data formatting | bytes 8847360
  192.5 0.0 copy-done
  192.5 0.7 copy.12
Async XLA Ops:
  187.9 4.7 %copy-start = (bf16[64,1280]{1,0:T(8,128)(2,1)S(1)}, bf16[64,1280]{1,0:T(8,128)(2,1)}, u32[]{:S(2)}) copy-start(bf16[64,1280]{1,0:T(8,128)(2,1)} %get-tuple-element.5) | copy-start | bytes 491524

commit v2 on v1

--- a/solution.py
+++ b/solution.py
@@ -18,8 +18,8 @@
 
 
 def kernel(
-    chunks, acts_in, w_in, labels, protos, merged_out, out,
-    acts, w, asq_t, target, part, part_in, row_sum, z_send, z_in, gsq, nd, nd_in, nd_sum,
+    chunks, acts_in, w_in, labels_in, protos_in, merged_out, out,
+    labels, protos, acts_t, acts, w, asq_t, target, part, part_in, row_sum, z_send, z_in, gsq, nd, nd_in, nd_sum,
     far_in, near_in, sum_in, merged, part2, part2_in, row_sum2, z_send2, z_in2,
     send_sem, recv_sem, gather_send, gather_recv, local_sem, store_sem,
 ):
@@ -107,14 +107,19 @@
             merged.at[c], merged_out.at[:, pl.ds(pl.multiple_of(c * CW, CW), CW)], store_sem.at[c]
         )
 
-    own = rows_of(y, block)
-    load_acts = pltpu.make_async_copy(acts_in, acts.at[own], local_sem.at[chunks])
+    load_acts = pltpu.make_async_copy(acts_in, acts_t.at[y], local_sem.at[chunks])
     load_acts.start()
     loads = [
         pltpu.make_async_copy(w_in.at[:, pl.ds(c * CW, CW)], w.at[c], local_sem.at[c]) for c in range(chunks)
     ]
     for load in loads:
         load.start()
+    small = [
+        pltpu.make_async_copy(labels_in, labels, local_sem.at[chunks + 1]),
+        pltpu.make_async_copy(protos_in, protos, local_sem.at[chunks + 2]),
+    ]
+    for load in small:
+        load.start()
 
     barrier = pltpu.get_barrier_semaphore()
     peers = [at_y(1), at_y(-1), at_x(1), at_x(2), at_x(3), pair, twin, at_z(1), at_z(-1)]
@@ -122,38 +127,58 @@
         pl.semaphore_signal(barrier, inc=1, device_id=peer, device_id_type=MESH)
     pl.semaphore_wait(barrier, len(peers))
 
-    def gather(src, index, slot, device):
+    pieces = [pl.ds(0, units // 2), pl.ds(units // 2, units // 2)]
+
+    def gather(src, index, slot, h, device):
         return pltpu.make_async_remote_copy(
-            src_ref=src, dst_ref=acts.at[rows_of(index, block)], send_sem=gather_send.at[slot],
-            recv_sem=gather_recv.at[slot], device_id=device, device_id_type=MESH,
+            src_ref=src.at[pieces[h]], dst_ref=acts_t.at[index, pieces[h]], send_sem=gather_send.at[slot, h],
+            recv_sem=gather_recv.at[slot, h], device_id=device, device_id_type=MESH,
         )
 
-    up, down = gather(acts_in, y, 0, at_y(1)), gather(acts_in, y, 1, at_y(-1))
-    up.start()
-    down.start()
-
+    up = [gather(acts_in, y, 0, h, at_y(1)) for h in range(2)]
+    down = [gather(acts_in, y, 1, h, at_y(-1)) for h in range(2)]
+    source = (y + 2 * core - 1 + YS) % YS
+    onward = [gather(acts_t.at[source], source, 2, h, at_y(1 - 2 * core)) for h in range(2)]
+    for h in range(2):
+        up[h].start()
+        down[h].start()
+
+    def tokens(index):
+        rows = rows_of(index, block)
+        turned = acts_t[index]
+        acts[rows, :] = turned.T
+        wide = turned.astype(F32)
+        asq_t[:, rows] = (wide * wide).astype(BF16)
+        step = (index - x + XS) % XS
+
+        @pl.loop(0, chunks)
+        def _(c):
+            part[c, rows, :] = jnp.dot(acts[rows, :], w[c], preferred_element_type=F32).astype(BF16)
+
+            @pl.when(step != 0)
+            def _():
+                x1(c, step).start()
+
+    for load in small:
+        load.wait()
     onehot = (
-        labels[rows_of(row, half), :] == lax.broadcasted_iota(jnp.int32, (half, protos.shape[0]), 1)
+        labels[:, rows_of(x, block)] == lax.broadcasted_iota(jnp.int32, (protos.shape[0], block), 0)
     ).astype(F32).astype(BF16)
-    target[...] = jnp.dot(onehot, protos[...], preferred_element_type=F32)
-
-    def square(index):
-        wide = acts[rows_of(index, block), :].astype(F32)
-        asq_t[:, rows_of(index, block)] = (wide * wide).T.astype(BF16)
+    target[...] = lax.dot_general(onehot, protos[...], (((0,), (0,)), ((), ())), preferred_element_type=F32)
 
     load_acts.wait()
-    square(y)
-    up.wait_recv()
-    down.wait_recv()
-    source = (y + 2 * core - 1 + YS) % YS
-    onward = gather(acts.at[rows_of(source, block)], source, 2, at_y(1 - 2 * core))
-    onward.start()
-    square((y + 1) % YS)
-    square((y + 3) % YS)
-    onward.wait_recv()
-    square((y + 2) % YS)
     for load in loads:
         load.wait()
+    tokens(y)
+    for h in range(2):
+        up[h].wait_recv()
+        down[h].wait_recv()
+        onward[h].start()
+    tokens((y + 1) % YS)
+    tokens((y + 3) % YS)
+    for h in range(2):
+        onward[h].wait_recv()
+    tokens((y + 2) % YS)
 
     def product(left, c, right, result):
         for m in range(2):
@@ -167,11 +192,6 @@
             total = total + arrived[c, d, rows, :].astype(F32)
         return total
 
-    def s1(c):
-        product(acts, c, w, part)
-        for d in (1, 2, 3):
-            x1(c, d).start()
-
     def s2(c):
         for d in (1, 2, 3):
             x1(c, d).wait_recv()
@@ -181,7 +201,7 @@
 
     def s3(c):
         z1(c).wait_recv()
-        grad = row_sum[c] + z_in[c].astype(F32) - target[:, pl.ds(pl.multiple_of(c * CW, CW), CW)]
+        grad = row_sum[c] + z_in[c].astype(F32) - target[rows_of(zl, half), pl.ds(pl.multiple_of(c * CW, CW), CW)]
         gsq[c, rows_of(row, half), :] = (grad * grad).astype(BF16)
         z2(c).start()
 
@@ -269,7 +289,7 @@
         z3(c).wait_recv()
         out[:, pl.ds(pl.multiple_of(c * CW, CW), CW)] = (row_sum2[c] + z_in2[c].astype(F32)).astype(BF16)
 
-    stages = [s1, s2, s3, s4, s5, s6, s7, s8, s9, s10, s11, s12, s13]
+    stages = [s2, s3, s4, s5, s6, s7, s8, s9, s10, s11, s12, s13]
 
     @pl.loop(0, chunks + len(stages) - 1)
     def _(tick):
@@ -280,9 +300,9 @@
             def _():
                 stages[k](c)
 
-    up.wait_send()
-    down.wait_send()
-    onward.wait_send()
+    for h in range(2):
+        for copy in (up, down, onward):
+            copy[h].wait_send()
 
     @pl.loop(0, chunks)
     def _(c):
@@ -301,7 +321,7 @@
 
 
 def local(activations, weights, labels, prototypes):
-    shard, units = activations.shape[1:]
+    units = activations.shape[2]
     tok, wide = labels.shape[1], weights.shape[2]
     chunks, block, half, piece = wide // CW, tok // XS, tok // XS // 2, units // ZH
 
@@ -316,13 +336,16 @@
             jax.ShapeDtypeStruct((units, wide), BF16),
             jax.ShapeDtypeStruct((half, wide), BF16),
         ),
-        in_specs=[anywhere, anywhere, inside, inside],
+        in_specs=[anywhere] * 4,
         out_specs=(anywhere, inside),
         scratch_shapes=[
+            vmem(1, tok, kind=jnp.int32),
+            vmem(prototypes.shape[1], wide),
+            vmem(YS, units, tok // YS),
             vmem(tok, units),
             vmem(chunks, units, CW),
             vmem(units, tok),
-            vmem(half, wide, kind=F32),
+            vmem(block, wide, kind=F32),
             vmem(chunks, tok, CW),
             vmem(chunks, XS - 1, block, CW),
             vmem(chunks, half, CW, kind=F32),
@@ -343,15 +366,15 @@
             vmem(chunks, half, CW),
             pltpu.SemaphoreType.DMA((chunks, SLOTS)),
             pltpu.SemaphoreType.DMA((chunks, SLOTS)),
-            pltpu.SemaphoreType.DMA((3,)),
-            pltpu.SemaphoreType.DMA((3,)),
-            pltpu.SemaphoreType.DMA((chunks + 1,)),
+            pltpu.SemaphoreType.DMA((3, 2)),
+            pltpu.SemaphoreType.DMA((3, 2)),
+            pltpu.SemaphoreType.DMA((chunks + 3,)),
             pltpu.SemaphoreType.DMA((chunks,)),
         ],
         compiler_params=pltpu.CompilerParams(
             collective_id=0, has_side_effects=True, vmem_limit_bytes=60 << 20
         ),
-    )(activations[0], weights[0], labels.reshape(tok, 1), prototypes[0])
+    )(activations[0].T, weights[0], labels, prototypes[0])
     return merged, result[None]
 
 

time: 197 us -> 189 us (0.959)
  the two profiles are of different devices: /device:TPU:8 before, /device:TPU:16 now
where the time goes in v2:
time: 189 us
  Pallas kernels  183 us (97%)
  local copies, waits for them, and re-layouts  5.33 us (3%)
    pallas_call x1, Pallas kernels, local(): pl.pallas_call(functools.partial(kernel, chunks), out_shape=(jax.ShapeDty...  183 us
    unnamed x4, local copies, waits for them, and re-layouts  5.33 us

profile of v2, /device:TPU:16, one launch (start us, length us, event | category | flops | bytes accessed | tf_op | source)
XLA Modules:
  0.0 188.8 jit_solution(18101389278534977308)
XLA Ops:
  0.6 182.8 %shard_map.59 = (bf16[1728,1280]{1,0:T(8,128)(2,1)}, bf16[64,1280]{1,0:T(8,128)(2,1)}) custom-call(bf16[1728,128]{1,0:T(8,128)(2,1)} %bitcast.7, bf16[1728,1280]{1,0:T(8,128)(2,1)} %bitcast.6, s32[1,512]{1,0:T(1,128)} %labels_in.1, bf16[128,1280]{1,0:T(8,128)(2,1)} %bitcast.8), custom_call_target="tpu_custom_call" | custom-call | tf_op jit(solution)/shard_map/pallas_call | solution.py:333
  183.5 0.0 copy-start
  183.5 4.7 %copy.8 = bf16[1728,1280]{1,0:T(8,128)(2,1)} copy(bf16[1728,1280]{1,0:T(8,128)(2,1)} %get-tuple-element.8) | data formatting | bytes 8847360
  188.2 0.0 copy-done
  188.2 0.7 copy.9
Async XLA Ops:
  183.5 4.7 %copy-start = (bf16[64,1280]{1,0:T(8,128)(2,1)S(1)}, bf16[64,1280]{1,0:T(8,128)(2,1)}, u32[]{:S(2)}) copy-start(bf16[64,1280]{1,0:T(8,128)(2,1)} %get-tuple-element.5) | copy-start | bytes 491524

commit v3 on v2

--- a/solution.py
+++ b/solution.py
@@ -13,15 +13,16 @@
 CW = 256
 HALF = CW // 2
 
-X1, Z1, Z2, X2, CORE, FAR, NEAR, SUM, MERGED, FORWARD, SHARE, X3, Z3 = 0, 3, 4, 5, 8, 9, 11, 13, 15, 17, 18, 22, 25
-SLOTS = 26
+X1, Z1, Z2, X2, CORE, PLAIN, FAR, NEAR, SUM, MERGED, FORWARD, SHARE, X3, Z3 = 0, 3, 4, 5, 8, 9, 10, 11, 12, 13, 15, 16, 20, 23
+G_Z, G_ON, G_PAIR, G_X = 24, 26, 27, 28
+SLOTS = 31
 
 
 def kernel(
     chunks, acts_in, w_in, labels_in, protos_in, merged_out, out,
-    labels, protos, acts_t, acts, w, asq_t, target, part, part_in, row_sum, z_send, z_in, gsq, nd, nd_in, nd_sum,
-    far_in, near_in, sum_in, merged, part2, part2_in, row_sum2, z_send2, z_in2,
-    send_sem, recv_sem, gather_send, gather_recv, local_sem, store_sem,
+    labels, protos, acts_t, acts, w, asq_t, target, part, part_in, row_sum, z_send, z_in, gsq, quarter, asq_q, plain, plain_out, plain_in,
+    nd, nd_in, nd_sum, far_in, near_in, sum_in, merged, part2, part2_in, row_sum2, z_send2, z_in2,
+    send_sem, recv_sem, gather_send, gather_recv, early_send, early_recv, local_sem, store_sem,
 ):
     task, row, y = lax.axis_index("task"), lax.axis_index("row"), lax.axis_index("col")
     zh, core = task // 2, task % 2
@@ -40,6 +41,8 @@
     def at_z(step):
         return {"task": (zh + step + ZH) % ZH * 2 + core}
 
+    way = 1 - 2 * core
+
     def at_y(step):
         return {"col": (y + step + YS) % YS}
 
@@ -65,32 +68,51 @@
         return remote(z_send.at[c], z_in.at[c], c, Z1, pair)
 
     def z2(c):
-        here = gsq.at[c, rows_of(row, half)]
+        here = gsq.at[c, 0, rows_of(row, half)]
         return remote(here, here, c, Z2, pair)
 
     def x2(c, d):
-        here = gsq.at[c, rows_of(x, block)]
+        here = gsq.at[c, 0, rows_of(x, block)]
         return remote(here, here, c, X2 + d - 1, at_x(d))
 
+    def g_z(c, k):
+        rows = rows_of(row, half)
+        return remote(gsq.at[c, 0, rows], gsq.at[c, 3 - 2 * k, rows], c, G_Z + k, at_z(1 - 2 * k))
+
+    def g_on(c):
+        rows = rows_of(row, half)
+        return remote(gsq.at[c, 3 - 2 * core, rows], gsq.at[c, 2, rows], c, G_ON, at_z(way))
+
+    def g_pair(c):
+        here = gsq.at[c, pl.ds(1, ZH - 1), rows_of(row, half)]
+        return remote(here, here, c, G_PAIR, pair)
+
+    def g_x(c, d):
+        here = gsq.at[c, pl.ds(1, ZH - 1), rows_of(x, block)]
+        return remote(here, here, c, G_X + d - 1, at_x(d))
+
     def across(c):
-        return remote(nd.at[c, :, :, others], nd_in.at[c], c, CORE, twin)
-
-    def far(c, k):
-        return remote(nd_sum.at[c, k, z_piece(2)], far_in.at[c, k], c, FAR + k, at_z(1 - 2 * k))
-
-    def near(c, k):
-        return remote(nd_sum.at[c, 1 - k, z_piece(1 - 2 * k)], near_in.at[c, k], c, NEAR + k, at_z(1 - 2 * k))
-
-    def summed(c, k):
-        return remote(nd_sum.at[c, k, z_piece(1 - 2 * k)], sum_in.at[c, k], c, SUM + k, at_z(1 - 2 * k))
+        return remote(nd.at[c, :, others], nd_in.at[c], c, CORE, twin)
+
+    def across_plain(c):
+        return remote(plain_out.at[c, :, others], plain_in.at[c], c, PLAIN, twin)
+
+    def far(c):
+        return remote(nd_sum.at[c, z_piece(2)], far_in.at[c], c, FAR, at_z(way))
+
+    def near(c):
+        return remote(nd_sum.at[c, z_piece(-way)], near_in.at[c], c, NEAR, at_z(-way))
+
+    def summed(c):
+        return remote(nd_sum.at[c, z_piece(way)], sum_in.at[c], c, SUM, at_z(way))
 
     def spread(c, k):
         here = merged.at[c, z_piece(0), mine]
         return remote(here, here, c, MERGED + k, at_z(1 - 2 * k))
 
     def forward(c):
-        here = merged.at[c, z_piece(2 * core - 1), mine]
-        return remote(here, here, c, FORWARD, at_z(1 - 2 * core))
+        here = merged.at[c, z_piece(-way), mine]
+        return remote(here, here, c, FORWARD, at_z(way))
 
     def share(c, step):
         here = merged.at[c, z_piece(step), mine]
@@ -122,7 +144,7 @@
         load.start()
 
     barrier = pltpu.get_barrier_semaphore()
-    peers = [at_y(1), at_y(-1), at_x(1), at_x(2), at_x(3), pair, twin, at_z(1), at_z(-1)]
+    peers = [at(step) for at in (at_x, at_y, at_z) for step in (1, 2, 3)] + [pair, twin]
     for peer in peers:
         pl.semaphore_signal(barrier, inc=1, device_id=peer, device_id_type=MESH)
     pl.semaphore_wait(barrier, len(peers))
@@ -142,6 +164,17 @@
     for h in range(2):
         up[h].start()
         down[h].start()
+
+    def early(src, dst, slot, device):
+        return pltpu.make_async_remote_copy(
+            src_ref=src, dst_ref=dst, send_sem=early_send.at[slot], recv_sem=early_recv.at[slot],
+            device_id=device, device_id_type=MESH,
+        )
+
+    over_z = [early(acts_in.at[z_piece(k)], quarter.at[y, ZH - 1 - k], k - 1, at_z(k)) for k in (1, 2, 3)]
+    over_y = [early(quarter.at[y], quarter.at[y], 2 + d, at_y(d)) for d in (1, 2, 3)]
+    for copy in over_z:
+        copy.start()
 
     def tokens(index):
         rows = rows_of(index, block)
@@ -174,6 +207,10 @@
         up[h].wait_recv()
         down[h].wait_recv()
         onward[h].start()
+    for copy in over_z:
+        copy.wait_recv()
+    for copy in over_y:
+        copy.start()
     tokens((y + 1) % YS)
     tokens((y + 3) % YS)
     for h in range(2):
@@ -202,58 +239,79 @@
     def s3(c):
         z1(c).wait_recv()
         grad = row_sum[c] + z_in[c].astype(F32) - target[rows_of(zl, half), pl.ds(pl.multiple_of(c * CW, CW), CW)]
-        gsq[c, rows_of(row, half), :] = (grad * grad).astype(BF16)
+        gsq[c, 0, rows_of(row, half), :] = (grad * grad).astype(BF16)
         z2(c).start()
+        for k in range(2):
+            g_z(c, k).start()
 
     def s4(c):
         z2(c).wait_recv()
         for d in (1, 2, 3):
             x2(c, d).start()
+        for k in range(2):
+            g_z(c, k).wait_recv()
+        g_on(c).start()
 
     def s5(c):
         for d in (1, 2, 3):
             x2(c, d).wait_recv()
         for q in range(ZH):
             rows = pl.ds(q * piece, piece)
-            fisher = jnp.dot(asq_t[rows, :], gsq[c], preferred_element_type=F32)
-            nd[c, 0, rows, :] = (fisher * w[c, rows, :].astype(F32)).astype(BF16)
-            nd[c, 1, rows, :] = fisher.astype(BF16)
+            fisher = jnp.dot(asq_t[rows, :], gsq[c, 0], preferred_element_type=F32)
+            nd[c, rows, :] = (fisher * w[c, rows, :].astype(F32)).astype(BF16)
         across(c).start()
+        g_on(c).wait_recv()
+        g_pair(c).start()
 
     def s6(c):
         across(c).wait_recv()
 
-        def add(k, step):
+        def add(step):
             rows = z_piece(step)
-            nd_sum[c, k, rows, :] = (nd[c, k, rows, mine].astype(F32) + nd_in[c, k, rows, :].astype(F32)).astype(BF16)
-
-        add(0, 2)
-        far(c, 0).start()
-        add(1, 2)
-        far(c, 1).start()
-        add(1, 1)
-        near(c, 0).start()
-        add(0, -1)
-        near(c, 1).start()
-        add(0, 1)
-        add(1, -1)
-        add(0, 0)
-        add(1, 0)
+            nd_sum[c, rows, :] = (nd[c, rows, mine].astype(F32) + nd_in[c, rows, :].astype(F32)).astype(BF16)
+
+        add(2)
+        far(c).start()
+        add(-way)
+        near(c).start()
+        add(way)
+        add(0)
+        g_pair(c).wait_recv()
+        for d in (1, 2, 3):
+            g_x(c, d).start()
 
     def s7(c):
-        for k in range(2):
-            far(c, k).wait_recv()
-            rows = z_piece(1 - 2 * k)
-            nd_sum[c, k, rows, :] = (nd_sum[c, k, rows, :].astype(F32) + far_in[c, k].astype(F32)).astype(BF16)
-            summed(c, k).start()
+        far(c).wait_recv()
+        rows = z_piece(way)
+        nd_sum[c, rows, :] = (nd_sum[c, rows, :].astype(F32) + far_in[c].astype(F32)).astype(BF16)
+        summed(c).start()
+
+        @pl.when(c == 0)
+        def _():
+            for copy in over_y:
+                copy.wait_recv()
+
+            @pl.loop(0, YS)
+            def _(b):
+                for k in range(ZH - 1):
+                    wide = quarter[b, k].astype(F32)
+                    asq_q[k, :, rows_of(b, block)] = (wide * wide).astype(BF16)
+
+        for d in (1, 2, 3):
+            g_x(c, d).wait_recv()
+        total = jnp.dot(asq_t[z_piece(0), :], gsq[c, 0], preferred_element_type=F32)
+        for k in range(1, ZH):
+            total = total + jnp.dot(asq_q[k - 1], gsq[c, k], preferred_element_type=F32)
+        plain[c] = total
+        plain_out[c] = total.astype(BF16)
+        across_plain(c).start()
 
     def s8(c):
-        for k in range(2):
-            near(c, k).wait_recv()
-            summed(c, k).wait_recv()
+        for copy in (near, summed, across_plain):
+            copy(c).wait_recv()
         rows = z_piece(0)
-        numer = nd_sum[c, 0, rows, :].astype(F32) + near_in[c, 1].astype(F32) + sum_in[c, 0].astype(F32)
-        denom = nd_sum[c, 1, rows, :].astype(F32) + near_in[c, 0].astype(F32) + sum_in[c, 1].astype(F32)
+        numer = nd_sum[c, rows, :].astype(F32) + near_in[c].astype(F32) + sum_in[c].astype(F32)
+        denom = plain[c, :, mine] + plain_in[c].astype(F32)
         merged[c, rows, mine] = (numer / (denom + 1e-6)).astype(BF16)
         spread(c, 0).start()
         spread(c, 1).start()
@@ -303,6 +361,8 @@
     for h in range(2):
         for copy in (up, down, onward):
             copy[h].wait_send()
+    for copy in over_z + over_y:
+        copy.wait_send()
 
     @pl.loop(0, chunks)
     def _(c):
@@ -310,11 +370,12 @@
             x1(c, d).wait_send()
             x2(c, d).wait_send()
             x3(c, d).wait_send()
-        for copy in (z1, z2, z3, across, forward):
+            g_x(c, d).wait_send()
+        for copy in (z1, z2, z3, across, across_plain, far, near, summed, forward, g_on, g_pair):
             copy(c).wait_send()
         for k in range(2):
-            for copy in (far, near, summed, spread):
-                copy(c, k).wait_send()
+            spread(c, k).wait_send()
+            g_z(c, k).wait_send()
         for step in range(ZH):
             share(c, step).wait_send()
         store(c).wait()
@@ -351,13 +412,18 @@
             vmem(chunks, half, CW, kind=F32),
             vmem(chunks, half, CW),
             vmem(chunks, half, CW),
-            vmem(chunks, tok, CW),
-            vmem(chunks, 2, units, CW),
-            vmem(chunks, 2, units, HALF),
-            vmem(chunks, 2, units, HALF),
-            vmem(chunks, 2, piece, HALF),
-            vmem(chunks, 2, piece, HALF),
-            vmem(chunks, 2, piece, HALF),
+            vmem(chunks, ZH, tok, CW),
+            vmem(YS, ZH - 1, piece, tok // YS),
+            vmem(ZH - 1, piece, tok),
+            vmem(chunks, piece, CW, kind=F32),
+            vmem(chunks, piece, CW),
+            vmem(chunks, piece, HALF),
+            vmem(chunks, units, CW),
+            vmem(chunks, units, HALF),
+            vmem(chunks, units, HALF),
+            vmem(chunks, piece, HALF),
+            vmem(chunks, piece, HALF),
+            vmem(chunks, piece, HALF),
             vmem(chunks, units, CW),
             vmem(chunks, tok, CW),
             vmem(chunks, XS - 1, block, CW),
@@ -368,6 +434,8 @@
             pltpu.SemaphoreType.DMA((chunks, SLOTS)),
             pltpu.SemaphoreType.DMA((3, 2)),
             pltpu.SemaphoreType.DMA((3, 2)),
+            pltpu.SemaphoreType.DMA((6,)),
+            pltpu.SemaphoreType.DMA((6,)),
             pltpu.SemaphoreType.DMA((chunks + 3,)),
             pltpu.SemaphoreType.DMA((chunks,)),
         ],

time: 189 us -> 177 us (0.937)
  the two profiles are of different devices: /device:TPU:16 before, /device:TPU:8 now
where the time goes in v3:
time: 177 us
  Pallas kernels  171 us (97%)
  local copies, waits for them, and re-layouts  5.33 us (3%)
    pallas_call x1, Pallas kernels, local(): pl.pallas_call(functools.partial(kernel, chunks), out_shape=(jax.ShapeDty...  171 us
    unnamed x4, local copies, waits for them, and re-layouts  5.33 us

profile of v3, /device:TPU:8, one launch (start us, length us, event | category | flops | bytes accessed | tf_op | source)
XLA Modules:
  0.0 176.9 jit_solution(5624060948530379125)
XLA Ops:
  0.6 170.9 %shard_map.59 = (bf16[1728,1280]{1,0:T(8,128)(2,1)}, bf16[64,1280]{1,0:T(8,128)(2,1)}) custom-call(bf16[1728,128]{1,0:T(8,128)(2,1)} %bitcast.7, bf16[1728,1280]{1,0:T(8,128)(2,1)} %bitcast.6, s32[1,512]{1,0:T(1,128)} %labels_in.1, bf16[128,1280]{1,0:T(8,128)(2,1)} %bitcast.8), custom_call_target="tpu_custom_call" | custom-call | tf_op jit(solution)/shard_map/pallas_call | solution.py:394
  171.5 0.0 copy-start
  171.5 4.7 %copy.8 = bf16[1728,1280]{1,0:T(8,128)(2,1)} copy(bf16[1728,1280]{1,0:T(8,128)(2,1)} %get-tuple-element.8) | data formatting | bytes 8847360
  176.2 0.0 copy-done
  176.2 0.7 copy.9
Async XLA Ops:
  171.5 4.7 %copy-start = (bf16[64,1280]{1,0:T(8,128)(2,1)S(1)}, bf16[64,1280]{1,0:T(8,128)(2,1)}, u32[]{:S(2)}) copy-start(bf16[64,1280]{1,0:T(8,128)(2,1)} %get-tuple-element.5) | copy-start | bytes 491524

commit v4 on v3

--- a/solution.py
+++ b/solution.py
@@ -13,20 +13,22 @@
 CW = 256
 HALF = CW // 2
 
-X1, Z1, Z2, X2, CORE, PLAIN, FAR, NEAR, SUM, MERGED, FORWARD, SHARE, X3, Z3 = 0, 3, 4, 5, 8, 9, 10, 11, 12, 13, 15, 16, 20, 23
-G_Z, G_ON, G_PAIR, G_X = 24, 26, 27, 28
-SLOTS = 31
+X1, Z1, X2, CORE, PLAIN, FAR, NEAR, SUM, MERGED, FORWARD, SHARE, X3, Z3 = 0, 3, 4, 7, 8, 9, 10, 11, 12, 14, 15, 19, 22
+RING, RING_END, G_X = 23, 29, 30
+SLOTS = 39
 
 
 def kernel(
     chunks, acts_in, w_in, labels_in, protos_in, merged_out, out,
     labels, protos, acts_t, acts, w, asq_t, target, part, part_in, row_sum, z_send, z_in, gsq, quarter, asq_q, plain, plain_out, plain_in,
-    nd, nd_in, nd_sum, far_in, near_in, sum_in, merged, part2, part2_in, row_sum2, z_send2, z_in2,
+    w_early, weighted, weighted_out, weighted_in, nd, nd_in, nd_sum, far_in, near_in, sum_in, merged, part2, part2_in, row_sum2, z_send2, z_in2,
     send_sem, recv_sem, gather_send, gather_recv, early_send, early_recv, local_sem, store_sem,
 ):
     task, row, y = lax.axis_index("task"), lax.axis_index("row"), lax.axis_index("col")
     zh, core = task // 2, task % 2
     x, zl = row // 2, row % 2
+    place = zh * 2 + zl
+    last = chunks - 1
     tok, units = acts.shape
     block = tok // XS
     half = block // 2
@@ -67,32 +69,37 @@
     def z1(c):
         return remote(z_send.at[c], z_in.at[c], c, Z1, pair)
 
-    def z2(c):
-        here = gsq.at[c, 0, rows_of(row, half)]
-        return remote(here, here, c, Z2, pair)
+    def ring(step):
+        spot = (place + step + 2 * ZH) % (2 * ZH)
+        return spot // 2, x * 2 + spot % 2
+
+    def at_ring(step):
+        z, r = ring(step)
+        return {"task": z * 2 + core, "row": r}
+
+    def pass_on(c, hop, k):
+        z, r = ring((2 * k - 1) * (hop - 1))
+        here = gsq.at[c, z, rows_of(r, half)]
+        return remote(here, here, c, RING + 2 * (hop - 1) + k, at_ring(1 - 2 * k))
+
+    def pass_last(c):
+        z, r = ring(-3 * way)
+        here = gsq.at[c, z, rows_of(r, half)]
+        return remote(here, here, c, RING_END, at_ring(way))
 
     def x2(c, d):
-        here = gsq.at[c, 0, rows_of(x, block)]
+        here = gsq.at[c, zh, rows_of(x, block)]
         return remote(here, here, c, X2 + d - 1, at_x(d))
 
-    def g_z(c, k):
-        rows = rows_of(row, half)
-        return remote(gsq.at[c, 0, rows], gsq.at[c, 3 - 2 * k, rows], c, G_Z + k, at_z(1 - 2 * k))
-
-    def g_on(c):
-        rows = rows_of(row, half)
-        return remote(gsq.at[c, 3 - 2 * core, rows], gsq.at[c, 2, rows], c, G_ON, at_z(way))
-
-    def g_pair(c):
-        here = gsq.at[c, pl.ds(1, ZH - 1), rows_of(row, half)]
-        return remote(here, here, c, G_PAIR, pair)
-
-    def g_x(c, d):
-        here = gsq.at[c, pl.ds(1, ZH - 1), rows_of(x, block)]
-        return remote(here, here, c, G_X + d - 1, at_x(d))
+    def g_x(c, k, d):
+        here = gsq.at[c, (zh + k) % ZH, rows_of(x, block)]
+        return remote(here, here, c, G_X + 3 * (k - 1) + d - 1, at_x(d))
 
     def across(c):
         return remote(nd.at[c, :, others], nd_in.at[c], c, CORE, twin)
+
+    def across_weighted(c):
+        return remote(weighted_out.at[:, others], weighted_in, c, CORE, twin)
 
     def across_plain(c):
         return remote(plain_out.at[c, :, others], plain_in.at[c], c, PLAIN, twin)
@@ -144,7 +151,7 @@
         load.start()
 
     barrier = pltpu.get_barrier_semaphore()
-    peers = [at(step) for at in (at_x, at_y, at_z) for step in (1, 2, 3)] + [pair, twin]
+    peers = [at(step) for at in (at_x, at_y, at_z) for step in (1, 2, 3)] + [at_ring(1), at_ring(-1), twin]
     for peer in peers:
         pl.semaphore_signal(barrier, inc=1, device_id=peer, device_id_type=MESH)
     pl.semaphore_wait(barrier, len(peers))
@@ -173,7 +180,10 @@
 
     over_z = [early(acts_in.at[z_piece(k)], quarter.at[y, ZH - 1 - k], k - 1, at_z(k)) for k in (1, 2, 3)]
     over_y = [early(quarter.at[y], quarter.at[y], 2 + d, at_y(d)) for d in (1, 2, 3)]
-    for copy in over_z:
+    weights_z = [
+        early(w_in.at[z_piece(k), pl.ds(last * CW, CW)], w_early.at[ZH - 1 - k], 5 + k, at_z(k)) for k in (1, 2, 3)
+    ]
+    for copy in over_z + weights_z:
         copy.start()
 
     def tokens(index):
@@ -239,53 +249,71 @@
     def s3(c):
         z1(c).wait_recv()
         grad = row_sum[c] + z_in[c].astype(F32) - target[rows_of(zl, half), pl.ds(pl.multiple_of(c * CW, CW), CW)]
-        gsq[c, 0, rows_of(row, half), :] = (grad * grad).astype(BF16)
-        z2(c).start()
-        for k in range(2):
-            g_z(c, k).start()
+        gsq[c, zh, rows_of(row, half), :] = (grad * grad).astype(BF16)
+        for k in range(2):
+            pass_on(c, 1, k).start()
 
     def s4(c):
-        z2(c).wait_recv()
+        for k in range(2):
+            pass_on(c, 1, k).wait_recv()
         for d in (1, 2, 3):
             x2(c, d).start()
         for k in range(2):
-            g_z(c, k).wait_recv()
-        g_on(c).start()
+            pass_on(c, 2, k).start()
 
     def s5(c):
         for d in (1, 2, 3):
             x2(c, d).wait_recv()
-        for q in range(ZH):
-            rows = pl.ds(q * piece, piece)
-            fisher = jnp.dot(asq_t[rows, :], gsq[c, 0], preferred_element_type=F32)
-            nd[c, rows, :] = (fisher * w[c, rows, :].astype(F32)).astype(BF16)
-        across(c).start()
-        g_on(c).wait_recv()
-        g_pair(c).start()
+
+        @pl.when(c != last)
+        def _():
+            for q in range(ZH):
+                rows = pl.ds(q * piece, piece)
+                fisher = jnp.dot(asq_t[rows, :], gsq[c, zh], preferred_element_type=F32)
+                nd[c, rows, :] = (fisher * w[c, rows, :].astype(F32)).astype(BF16)
+            across(c).start()
+
+        for k in range(2):
+            pass_on(c, 2, k).wait_recv()
+        for k in range(2):
+            pass_on(c, 3, k).start()
 
     def s6(c):
-        across(c).wait_recv()
-
-        def add(step):
-            rows = z_piece(step)
-            nd_sum[c, rows, :] = (nd[c, rows, mine].astype(F32) + nd_in[c, rows, :].astype(F32)).astype(BF16)
-
-        add(2)
-        far(c).start()
-        add(-way)
-        near(c).start()
-        add(way)
-        add(0)
-        g_pair(c).wait_recv()
-        for d in (1, 2, 3):
-            g_x(c, d).start()
+        @pl.when(c != last)
+        def _():
+            across(c).wait_recv()
+
+            def add(step):
+                rows = z_piece(step)
+                nd_sum[c, rows, :] = (nd[c, rows, mine].astype(F32) + nd_in[c, rows, :].astype(F32)).astype(BF16)
+
+            add(2)
+            far(c).start()
+            add(-way)
+            near(c).start()
+            add(way)
+            add(0)
+
+        for k in range(2):
+            pass_on(c, 3, k).wait_recv()
+        pass_last(c).start()
+        for k in (1, 3):
+            for d in (1, 2, 3):
+                g_x(c, k, d).start()
 
     def s7(c):
-        far(c).wait_recv()
-        rows = z_piece(way)
-        nd_sum[c, rows, :] = (nd_sum[c, rows, :].astype(F32) + far_in[c].astype(F32)).astype(BF16)
-        summed(c).start()
-
+        @pl.when(c != last)
+        def _():
+            far(c).wait_recv()
+            rows = z_piece(way)
+            nd_sum[c, rows, :] = (nd_sum[c, rows, :].astype(F32) + far_in[c].astype(F32)).astype(BF16)
+            summed(c).start()
+
+        pass_last(c).wait_recv()
+        for d in (1, 2, 3):
+            g_x(c, 2, d).start()
+
+    def s8(c):
         @pl.when(c == 0)
         def _():
             for copy in over_y:
@@ -297,22 +325,55 @@
                     wide = quarter[b, k].astype(F32)
                     asq_q[k, :, rows_of(b, block)] = (wide * wide).astype(BF16)
 
-        for d in (1, 2, 3):
-            g_x(c, d).wait_recv()
-        total = jnp.dot(asq_t[z_piece(0), :], gsq[c, 0], preferred_element_type=F32)
-        for k in range(1, ZH):
-            total = total + jnp.dot(asq_q[k - 1], gsq[c, k], preferred_element_type=F32)
-        plain[c] = total
-        plain_out[c] = total.astype(BF16)
-        across_plain(c).start()
-
-    def s8(c):
-        for copy in (near, summed, across_plain):
-            copy(c).wait_recv()
+        def fisher(k):
+            squares = asq_t[z_piece(0), :] if k == 0 else asq_q[k - 1]
+            return jnp.dot(squares, gsq[c, (zh + k) % ZH], preferred_element_type=F32)
+
+        for k in (1, 3, 2):
+            for d in (1, 2, 3):
+                g_x(c, k, d).wait_recv()
+
+        @pl.when(c != last)
+        def _():
+            total = fisher(0)
+            for k in range(1, ZH):
+                total = total + fisher(k)
+            plain[c] = total
+            plain_out[c] = total.astype(BF16)
+            across_plain(c).start()
+
+        @pl.when(c == last)
+        def _():
+            for copy in weights_z:
+                copy.wait_recv()
+            plain[c] = fisher(0)
+            weighted[...] = plain[c] * w[c, z_piece(0), :].astype(F32)
+            for k in range(1, ZH):
+                one = fisher(k)
+                plain[c] += one
+                weighted[...] += one * w_early[k - 1].astype(F32)
+            plain_out[c] = plain[c].astype(BF16)
+            weighted_out[...] = weighted[...].astype(BF16)
+            across_plain(c).start()
+            across_weighted(c).start()
+
+    def s8b(c):
+        across_plain(c).wait_recv()
         rows = z_piece(0)
-        numer = nd_sum[c, rows, :].astype(F32) + near_in[c].astype(F32) + sum_in[c].astype(F32)
-        denom = plain[c, :, mine] + plain_in[c].astype(F32)
-        merged[c, rows, mine] = (numer / (denom + 1e-6)).astype(BF16)
+        denom = plain[c, :, mine] + plain_in[c].astype(F32) + 1e-6
+
+        @pl.when(c != last)
+        def _():
+            near(c).wait_recv()
+            summed(c).wait_recv()
+            numer = nd_sum[c, rows, :].astype(F32) + near_in[c].astype(F32) + sum_in[c].astype(F32)
+            merged[c, rows, mine] = (numer / denom).astype(BF16)
+
+        @pl.when(c == last)
+        def _():
+            across_weighted(c).wait_recv()
+            merged[c, rows, mine] = ((weighted[:, mine] + weighted_in[...].astype(F32)) / denom).astype(BF16)
+
         spread(c, 0).start()
         spread(c, 1).start()
         share(c, 0).start()
@@ -347,7 +408,7 @@
         z3(c).wait_recv()
         out[:, pl.ds(pl.multiple_of(c * CW, CW), CW)] = (row_sum2[c] + z_in2[c].astype(F32)).astype(BF16)
 
-    stages = [s2, s3, s4, s5, s6, s7, s8, s9, s10, s11, s12, s13]
+    stages = [s2, s3, s4, s5, s6, s7, s8, s8b, s9, s10, s11, s12, s13]
 
     @pl.loop(0, chunks + len(stages) - 1)
     def _(tick):
@@ -361,7 +422,7 @@
     for h in range(2):
         for copy in (up, down, onward):
             copy[h].wait_send()
-    for copy in over_z + over_y:
+    for copy in over_z + over_y + weights_z:
         copy.wait_send()
 
     @pl.loop(0, chunks)
@@ -370,12 +431,24 @@
             x1(c, d).wait_send()
             x2(c, d).wait_send()
             x3(c, d).wait_send()
-            g_x(c, d).wait_send()
-        for copy in (z1, z2, z3, across, across_plain, far, near, summed, forward, g_on, g_pair):
+            for k in (1, 2, 3):
+                g_x(c, k, d).wait_send()
+        for copy in (z1, z3, across_plain, forward, pass_last):
             copy(c).wait_send()
         for k in range(2):
             spread(c, k).wait_send()
-            g_z(c, k).wait_send()
+            for hop in (1, 2, 3):
+                pass_on(c, hop, k).wait_send()
+
+        @pl.when(c != last)
+        def _():
+            for copy in (across, far, near, summed):
+                copy(c).wait_send()
+
+        @pl.when(c == last)
+        def _():
+            across_weighted(c).wait_send()
+
         for step in range(ZH):
             share(c, step).wait_send()
         store(c).wait()
@@ -418,6 +491,10 @@
             vmem(chunks, piece, CW, kind=F32),
             vmem(chunks, piece, CW),
             vmem(chunks, piece, HALF),
+            vmem(ZH - 1, piece, CW),
+            vmem(piece, CW, kind=F32),
+            vmem(piece, CW),
+            vmem(piece, HALF),
             vmem(chunks, units, CW),
             vmem(chunks, units, HALF),
             vmem(chunks, units, HALF),
@@ -434,8 +511,8 @@
             pltpu.SemaphoreType.DMA((chunks, SLOTS)),
             pltpu.SemaphoreType.DMA((3, 2)),
             pltpu.SemaphoreType.DMA((3, 2)),
-            pltpu.SemaphoreType.DMA((6,)),
-            pltpu.SemaphoreType.DMA((6,)),
+            pltpu.SemaphoreType.DMA((9,)),
+            pltpu.SemaphoreType.DMA((9,)),
             pltpu.SemaphoreType.DMA((chunks + 3,)),
             pltpu.SemaphoreType.DMA((chunks,)),
         ],

time: 177 us -> 157 us (0.89); the launches traced: 177 us -> 154 us
  Pallas kernels: 171 us -> 148 us
    pallas_call x1, Pallas kernels: 171 us -> 148 us  [local(): pl.pallas_call(functools.partial(kernel, chunks), out_shape=(jax.ShapeDty...]
where the time goes in v4:
time: 157 us; the launch traced here: 154 us
  Pallas kernels  148 us (94%)
  local copies, waits for them, and re-layouts  5.33 us (3%)
    pallas_call x1, Pallas kernels, local(): pl.pallas_call(functools.partial(kernel, chunks), out_shape=(jax.ShapeDty...  148 us
    unnamed x4, local copies, waits for them, and re-layouts  5.33 us

profile of v4, /device:TPU:8, one launch (start us, length us, event | category | flops | bytes accessed | tf_op | source)
XLA Modules:
  0.0 154.0 jit_solution(10467921978958923932)
XLA Ops:
  0.6 148.1 %shard_map.59 = (bf16[1728,1280]{1,0:T(8,128)(2,1)}, bf16[64,1280]{1,0:T(8,128)(2,1)}) custom-call(bf16[1728,128]{1,0:T(8,128)(2,1)} %bitcast.7, bf16[1728,1280]{1,0:T(8,128)(2,1)} %bitcast.6, s32[1,512]{1,0:T(1,128)} %labels_in.1, bf16[128,1280]{1,0:T(8,128)(2,1)} %bitcast.8), custom_call_target="tpu_custom_call" | custom-call | tf_op jit(solution)/shard_map/pallas_call | solution.py:467
  148.7 0.0 copy-start
  148.7 4.7 %copy.8 = bf16[1728,1280]{1,0:T(8,128)(2,1)} copy(bf16[1728,1280]{1,0:T(8,128)(2,1)} %get-tuple-element.8) | data formatting | bytes 8847360
  153.4 0.0 copy-done
  153.4 0.7 copy.9
Async XLA Ops:
  148.7 4.7 %copy-start = (bf16[64,1280]{1,0:T(8,128)(2,1)S(1)}, bf16[64,1280]{1,0:T(8,128)(2,1)}, u32[]{:S(2)}) copy-start(bf16[64,1280]{1,0:T(8,128)(2,1)} %get-tuple-element.5) | copy-start | bytes 491524

commit v5 on v4

--- a/solution.py
+++ b/solution.py
@@ -83,9 +83,9 @@
         return remote(here, here, c, RING + 2 * (hop - 1) + k, at_ring(1 - 2 * k))
 
     def pass_last(c):
-        z, r = ring(-3 * way)
+        z, r = ring(3 - 6 * zl)
         here = gsq.at[c, z, rows_of(r, half)]
-        return remote(here, here, c, RING_END, at_ring(way))
+        return remote(here, here, c, RING_END, at_ring(2 * zl - 1))
 
     def x2(c, d):
         here = gsq.at[c, zh, rows_of(x, block)]
@@ -156,7 +156,8 @@
         pl.semaphore_signal(barrier, inc=1, device_id=peer, device_id_type=MESH)
     pl.semaphore_wait(barrier, len(peers))
 
-    pieces = [pl.ds(0, units // 2), pl.ds(units // 2, units // 2)]
+    cut = (units // 2 + 127) // 128 * 128
+    pieces = [pl.ds(0, cut), pl.ds(cut, units - cut)]
 
     def gather(src, index, slot, h, device):
         return pltpu.make_async_remote_copy(
@@ -186,21 +187,21 @@
     for copy in over_z + weights_z:
         copy.start()
 
-    def tokens(index):
+    def turn(index, h):
         rows = rows_of(index, block)
-        turned = acts_t[index]
-        acts[rows, :] = turned.T
+        turned = acts_t[index, pieces[h]]
+        acts[rows, pieces[h]] = turned.T
         wide = turned.astype(F32)
-        asq_t[:, rows] = (wide * wide).astype(BF16)
+        asq_t[pieces[h], rows] = (wide * wide).astype(BF16)
+
+    def multiply(index, c):
+        rows = rows_of(index, block)
         step = (index - x + XS) % XS
-
-        @pl.loop(0, chunks)
-        def _(c):
-            part[c, rows, :] = jnp.dot(acts[rows, :], w[c], preferred_element_type=F32).astype(BF16)
-
-            @pl.when(step != 0)
-            def _():
-                x1(c, step).start()
+        part[c, rows, :] = jnp.dot(acts[rows, :], w[c], preferred_element_type=F32).astype(BF16)
+
+        @pl.when(step != 0)
+        def _():
+            x1(c, step).start()
 
     for load in small:
         load.wait()
@@ -212,20 +213,31 @@
     load_acts.wait()
     for load in loads:
         load.wait()
-    tokens(y)
+    turn(y, 0)
+    turn(y, 1)
+
+    @pl.loop(0, chunks)
+    def _(c):
+        multiply(y, c)
+
+    beside = [(y + 1) % YS, (y + 3) % YS]
+    across_y = (y + 2) % YS
     for h in range(2):
         up[h].wait_recv()
         down[h].wait_recv()
         onward[h].start()
+        for index in beside:
+            turn(index, h)
     for copy in over_z:
         copy.wait_recv()
+    for index in beside:
+        multiply(index, 0)
+    for h in range(2):
+        onward[h].wait_recv()
+        turn(across_y, h)
     for copy in over_y:
         copy.start()
-    tokens((y + 1) % YS)
-    tokens((y + 3) % YS)
-    for h in range(2):
-        onward[h].wait_recv()
-    tokens((y + 2) % YS)
+    multiply(across_y, 0)
 
     def product(left, c, right, result):
         for m in range(2):
@@ -238,6 +250,12 @@
         for d in range(XS - 1):
             total = total + arrived[c, d, rows, :].astype(F32)
         return total
+
+    def s1(c):
+        @pl.when(c > 0)
+        def _():
+            for index in beside + [across_y]:
+                multiply(index, c)
 
     def s2(c):
         for d in (1, 2, 3):
@@ -357,7 +375,7 @@
             across_plain(c).start()
             across_weighted(c).start()
 
-    def s8b(c):
+    def merge(c):
         across_plain(c).wait_recv()
         rows = z_piece(0)
         denom = plain[c, :, mine] + plain_in[c].astype(F32) + 1e-6
@@ -392,10 +410,44 @@
     def s11(c):
         for step in range(ZH):
             share(c, step).wait_recv()
+        store(c).start()
         product(acts, c, merged, part2)
         for d in (1, 2, 3):
             x3(c, d).start()
-        store(c).start()
+        sent(c)
+
+        @pl.when(c == 0)
+        def _():
+            for h in range(2):
+                for copy in (up, down, onward):
+                    copy[h].wait_send()
+            for copy in over_z + over_y + weights_z:
+                copy.wait_send()
+
+    def sent(c):
+        for d in (1, 2, 3):
+            x1(c, d).wait_send()
+            x2(c, d).wait_send()
+            for k in (1, 2, 3):
+                g_x(c, k, d).wait_send()
+        for copy in (z1, across_plain, forward, pass_last):
+            copy(c).wait_send()
+        for k in range(2):
+            spread(c, k).wait_send()
+            for hop in (1, 2, 3):
+                pass_on(c, hop, k).wait_send()
+
+        @pl.when(c != last)
+        def _():
+            for copy in (across, far, near, summed):
+                copy(c).wait_send()
+
+        @pl.when(c == last)
+        def _():
+            across_weighted(c).wait_send()
+
+        for step in range(ZH):
+            share(c, step).wait_send()
 
     def s12(c):
         for d in (1, 2, 3):
@@ -407,8 +459,12 @@
     def s13(c):
         z3(c).wait_recv()
         out[:, pl.ds(pl.multiple_of(c * CW, CW), CW)] = (row_sum2[c] + z_in2[c].astype(F32)).astype(BF16)
-
-    stages = [s2, s3, s4, s5, s6, s7, s8, s8b, s9, s10, s11, s12, s13]
+        for d in (1, 2, 3):
+            x3(c, d).wait_send()
+        z3(c).wait_send()
+        store(c).wait()
+
+    stages = [s1, s2, s3, s4, s5, s6, s7, s8, merge, s9, s10, s11, s12, s13]
 
     @pl.loop(0, chunks + len(stages) - 1)
     def _(tick):
@@ -418,40 +474,6 @@
             @pl.when((c >= 0) & (c < chunks))
             def _():
                 stages[k](c)
-
-    for h in range(2):
-        for copy in (up, down, onward):
-            copy[h].wait_send()
-    for copy in over_z + over_y + weights_z:
-        copy.wait_send()
-
-    @pl.loop(0, chunks)
-    def _(c):
-        for d in (1, 2, 3):
-            x1(c, d).wait_send()
-            x2(c, d).wait_send()
-            x3(c, d).wait_send()
-            for k in (1, 2, 3):
-                g_x(c, k, d).wait_send()
-        for copy in (z1, z3, across_plain, forward, pass_last):
-            copy(c).wait_send()
-        for k in range(2):
-            spread(c, k).wait_send()
-            for hop in (1, 2, 3):
-                pass_on(c, hop, k).wait_send()
-
-        @pl.when(c != last)
-        def _():
-            for copy in (across, far, near, summed):
-                copy(c).wait_send()
-
-        @pl.when(c == last)
-        def _():
-            across_weighted(c).wait_send()
-
-        for step in range(ZH):
-            share(c, step).wait_send()
-        store(c).wait()
 
 
 def local(activations, weights, labels, prototypes):

time: 157 us -> 156 us (level); the launches traced: 154 us -> 156 us
  Pallas kernels: 148 us -> 150 us
    pallas_call x1, Pallas kernels: 148 us -> 150 us  [local(): pl.pallas_call(functools.partial(kernel, chunks), out_shape=(jax.ShapeDty...]
where the time goes in v5:
time: 156 us
  Pallas kernels  150 us (96%)
  local copies, waits for them, and re-layouts  5.33 us (3%)
    pallas_call x1, Pallas kernels, local(): pl.pallas_call(functools.partial(kernel, chunks), out_shape=(jax.ShapeDty...  150 us
    unnamed x4, local copies, waits for them, and re-layouts  5.33 us

profile of v5, /device:TPU:8, one launch (start us, length us, event | category | flops | bytes accessed | tf_op | source)
XLA Modules:
  0.0 155.8 jit_solution(4768536833847022526)
XLA Ops:
  0.6 149.8 %shard_map.59 = (bf16[1728,1280]{1,0:T(8,128)(2,1)}, bf16[64,1280]{1,0:T(8,128)(2,1)}) custom-call(bf16[1728,128]{1,0:T(8,128)(2,1)} %bitcast.7, bf16[1728,1280]{1,0:T(8,128)(2,1)} %bitcast.6, s32[1,512]{1,0:T(1,128)} %labels_in.1, bf16[128,1280]{1,0:T(8,128)(2,1)} %bitcast.8), custom_call_target="tpu_custom_call" | custom-call | tf_op jit(solution)/shard_map/pallas_call | solution.py:489
  150.4 0.0 copy-start
  150.4 4.7 %copy.8 = bf16[1728,1280]{1,0:T(8,128)(2,1)} copy(bf16[1728,1280]{1,0:T(8,128)(2,1)} %get-tuple-element.8) | data formatting | bytes 8847360
  155.1 0.0 copy-done
  155.1 0.7 copy.9
Async XLA Ops:
  150.4 4.7 %copy-start = (bf16[64,1280]{1,0:T(8,128)(2,1)S(1)}, bf16[64,1280]{1,0:T(8,128)(2,1)}, u32[]{:S(2)}) copy-start(bf16[64,1280]{1,0:T(8,128)(2,1)} %get-tuple-element.5) | copy-start | bytes 491524

commit v6 on v5

--- a/solution.py
+++ b/solution.py
@@ -539,7 +539,7 @@
             pltpu.SemaphoreType.DMA((chunks,)),
         ],
         compiler_params=pltpu.CompilerParams(
-            collective_id=0, has_side_effects=True, vmem_limit_bytes=60 << 20
+            collective_id=0, has_side_effects=True, vmem_limit_bytes=48 << 20
         ),
     )(activations[0].T, weights[0], labels, prototypes[0])
     return merged, result[None]

time: 156 us -> 156 us (level)
    unnamed x4 -> x8, local copies, waits for them, and re-layouts: 5.33 us -> 5.42 us
where the time goes in v6:
time: 156 us; the launch traced here: 155 us
  Pallas kernels  149 us (96%)
  local copies, waits for them, and re-layouts  5.42 us (3%)
    pallas_call x1, Pallas kernels, local(): pl.pallas_call(functools.partial(kernel, chunks), out_shape=(jax.ShapeDty...  149 us
    unnamed x8, local copies, waits for them, and re-layouts  5.42 us

profile of v6, /device:TPU:8, one launch (start us, length us, event | category | flops | bytes accessed | tf_op | source)
XLA Modules:
  0.0 155.1 jit_solution(18389097528366414450)
XLA Ops:
  0.6 0.0 copy-start
  0.6 1.0 copy-done
  1.6 0.0 copy-start.1
  1.6 1.0 copy-done.1
  2.6 0.0 copy-start.2
  2.6 0.7 copy-done.2
  3.3 149.1 %shard_map.59 = (bf16[1728,1280]{1,0:T(8,128)(2,1)S(1)}, bf16[64,1280]{1,0:T(8,128)(2,1)S(1)}) custom-call(bf16[1728,128]{1,0:T(8,128)(2,1)S(1)} %bitcast.6, bf16[1728,1280]{1,0:T(8,128)(2,1)} %bitcast.9, s32[1,512]{1,0:T(1,128)S(1)} %copy-done.2, bf16[128,1280]{1,0:T(8,128)(2,1)S(1)} %bitcast.7), custom_call_target="tpu_custom_call" | custom-call | tf_op jit(solution)/shard_map/pallas_call | solution.py:489
  152.4 2.1 %copy.8 = bf16[1728,1280]{1,0:T(8,128)(2,1)} copy(bf16[1728,1280]{1,0:T(8,128)(2,1)S(1)} %get-tuple-element.8) | data formatting | bytes 8847360
  154.5 0.7 copy.9
Async XLA Ops:
  0.6 1.0 copy-start
  1.6 1.0 copy-start.1
  2.6 0.7 copy-start.2
